TPU v7x, 128 devices: a whole 4x4x4 slice. The times are simulated.
128 devices in a mesh: seq: 16 (over z, x), ctx: 8 (over y, core).
Axes of the slice: x: 4, y: 4, z: 4, core: 2. Of those that a mesh axis runs over, the one named last changes fastest.
Arguments:
- queries: bfloat16 [8192, 4096], P(('seq', 'ctx')), may hold values from -90 to 90
- stretch_kv: bfloat16 [2, 8192, 1024], P(None, ('seq', 'ctx')), may hold values from -4.1 to 4.1
- cache_kv: bfloat16 [1024, 2, 8, 128, 128], P('ctx', None, None, 'seq'), may hold values from -4 to 4
- vertical: int32 [32, 8], replicated, may hold values from 0 to 1023, as said below
- slash: int32 [32, 24], replicated, may hold values from 0 to 1023
- owner_map: int32 [1024], replicated, may hold values from 0 to 1023, as said below
Outputs:
- attended: bfloat16 [8192, 4096], P(('seq', 'ctx'))
Inputs may be any that keep to these rules, and one draw needn't show every extreme that they name: For every head the 8 vertical blocks and the blocks 1024 - 1 - s of its slash entries s are 32 distinct blocks; for every head exactly 12 of them have storage rows in one range g * 128 to (g + 1) * 128 - 1, and at most 3 in each other such range, with exactly 3 in some. `owner_map`: each storage row appears once.
All inputs are finite; a program needn't handle non-finite values.
Results may differ from a plain program's by a relative error of at most 0.0075.
Values may be sent and summed in bfloat16 or wider, within the bound.
A program may use at most 128 MiB of HBM per device.

v0:
```python
import jax
import jax.numpy as jnp
from jax import lax
from jax.sharding import PartitionSpec as P

H = 32
KVH = 8
HD = 128
BLK = 128
CAP = 12


masked_value = -1e30


def stretch_positions(rows, shard, tok_rows, n_ctx):
    return (rows // tok_rows * n_ctx + shard) * tok_rows + rows % tok_rows


def online_update(carry, scores, visible, mixing):
    running_max, running_sum, weighted = carry
    masked = jnp.where(visible, scores, masked_value)
    new_max = jnp.maximum(running_max, jnp.max(masked, axis=2, keepdims=True))
    weights = jnp.where(visible, jnp.exp(masked - new_max), 0.0)
    fading = jnp.exp(running_max - new_max)
    new_sum = running_sum * fading + jnp.sum(weights, axis=2, keepdims=True)
    new_weighted = weighted * fading + mixing(weights.astype(jnp.bfloat16))
    return (new_max, new_sum, new_weighted)


def owner_slots(owner, local_row, owner_group):
    owned = owner == owner_group
    slot_rank = jnp.cumsum(owned.astype(jnp.int32), axis=1) - 1
    slot_hit = owned[:, :, None] & (
        slot_rank[:, :, None] == jnp.arange(CAP, dtype=jnp.int32)[None, None, :]
    )
    slot_row = jnp.sum(jnp.where(slot_hit, local_row[:, :, None], 0), axis=1)
    return (slot_row, jnp.any(slot_hit, axis=1))


def on_device(queries, stretch_kv, cache_kv, vertical, slash, owner_map):
    n_seq = lax.axis_size("seq")
    n_ctx = lax.axis_size("ctx")
    seq_index = lax.axis_index("seq")
    ctx_index = lax.axis_index("ctx")
    tok_rows = queries.shape[0]
    per_device = H // n_seq
    query_rows = tok_rows * n_seq
    score_scale = HD ** (-0.5)
    sent_queries = queries.reshape(tok_rows, n_seq, per_device * HD)
    own_queries = lax.all_to_all(
        sent_queries, "seq", split_axis=1, concat_axis=0, tiled=True
    ).reshape(query_rows, per_device, HD)
    widened_kv = jnp.repeat(stretch_kv.reshape(2, tok_rows, KVH, HD), n_seq // KVH, axis=2)
    own_kv = lax.all_to_all(widened_kv, "seq", split_axis=2, concat_axis=1, tiled=True).reshape(
        2, query_rows, HD
    )
    row_index = jnp.arange(query_rows, dtype=jnp.int32)
    query_position = stretch_positions(row_index, ctx_index, tok_rows, n_ctx)
    start_carry = (
        jnp.full((per_device, query_rows, 1), masked_value, jnp.float32),
        jnp.zeros((per_device, query_rows, 1), jnp.float32),
        jnp.zeros((per_device, query_rows, HD), jnp.float32),
    )
    piece = lax.all_gather(own_kv, "ctx", axis=1, tiled=True)

    def visit(index, inner):
        shard_kv = lax.dynamic_slice_in_dim(piece, index * query_rows, query_rows, 1)
        key_position = stretch_positions(row_index, index, tok_rows, n_ctx)
        scores = (
            jnp.einsum("qpd,kd->pqk", own_queries, shard_kv[0], preferred_element_type=jnp.float32)
            * score_scale
        )
        visible = (key_position[None, :] <= query_position[:, None])[None]

        def stretch_mix(rounded):
            return jnp.einsum(
                "pqk,kd->pqd", rounded, shard_kv[1], preferred_element_type=jnp.float32
            )

        return online_update(inner, scores, visible, stretch_mix)

    carry = lax.fori_loop(0, piece.shape[1] // query_rows, visit, start_carry)
    blk_ctx = cache_kv.shape[0]
    part_rows = cache_kv.shape[3]
    total_blocks = blk_ctx * n_ctx
    selected = jnp.concatenate([vertical, total_blocks - 1 - slash], axis=1)
    storage = owner_map[selected]
    owner = storage // blk_ctx
    local_row = storage % blk_ctx
    send_rows, send_hit = owner_slots(owner, local_row, ctx_index)
    head_kv = jnp.arange(H, dtype=jnp.int32) // (H // KVH)

    def group_valid(owner_group):
        return owner_slots(owner, local_row, owner_group)[1]

    valid_all = jax.vmap(group_valid)(jnp.arange(n_ctx, dtype=jnp.int32))
    own_valid = lax.dynamic_slice_in_dim(valid_all, seq_index * per_device, per_device, 1)
    packed = cache_kv[send_rows, :, head_kv[:, None]]
    packed = packed.reshape(n_seq, per_device, CAP, 2, part_rows, HD)
    widened = jnp.broadcast_to(packed[:, None], (n_seq, n_ctx) + packed.shape[1:]).reshape(
        (n_seq * n_ctx, 1) + packed.shape[1:]
    )
    received = lax.all_to_all(widened, ("seq", "ctx"), split_axis=0, concat_axis=1, tiled=True)
    arranged = received.reshape((n_seq, n_ctx) + packed.shape[1:])
    arranged = jnp.transpose(arranged, (2, 1, 3, 4, 0, 5, 6)).reshape(
        per_device, n_ctx * CAP, 2, BLK, HD
    )
    fold_piece = arranged

    def visit(index, inner):
        blocks = lax.dynamic_slice_in_dim(fold_piece, index * CAP, CAP, 1)
        owner_group = 0 // CAP + index
        live_slots = lax.dynamic_index_in_dim(own_valid, owner_group, 0, keepdims=False)
        block_keys = blocks[:, :, 0].reshape(per_device, CAP * BLK, HD)
        block_values = blocks[:, :, 1].reshape(per_device, CAP * BLK, HD)
        scores = (
            jnp.einsum("qpd,pkd->pqk", own_queries, block_keys, preferred_element_type=jnp.float32)
            * score_scale
        )
        visible = jnp.repeat(live_slots, BLK, axis=1)[:, None, :]

        def block_mix(rounded):
            return jnp.einsum(
                "pqk,pkd->pqd", rounded, block_values, preferred_element_type=jnp.float32
            )

        return online_update(inner, scores, visible, block_mix)

    carry = lax.fori_loop(0, fold_piece.shape[1] // CAP, visit, carry)
    running_max, running_sum, weighted = carry
    attended = (weighted / running_sum).astype(jnp.bfloat16)
    outgoing = jnp.transpose(attended, (1, 0, 2)).reshape(n_seq, tok_rows, per_device * HD)
    returned = lax.all_to_all(outgoing, "seq", split_axis=0, concat_axis=2, tiled=True)
    return returned.reshape(tok_rows, H * HD)


def solution(mesh):
    placed = (
        P(("seq", "ctx"), None),
        P(None, ("seq", "ctx"), None),
        P("ctx", None, None, "seq", None),
        P(),
        P(),
        P(),
    )
    return jax.shard_map(
        on_device, mesh=mesh, in_specs=placed, out_specs=P(("seq", "ctx"), None), check_vma=False
    )
```

profile of v0, /device:TPU:0, one launch (start us, length us, event | category | flops | bytes accessed | tf_op | source)
XLA Modules:
  0.0 363.6 jit_solution(12740948286434524157)
XLA Ops:
  7.7 19.3 %all_to_all.54 = bf16[2,64,16,128]{3,1,0,2:T(8,128)(2,1)S(1)} all-to-all(bf16[2,64,16,128]{3,1,0,2:T(8,128)(2,1)S(1)} %bitcast.179), channel_id=1, replica_groups=mesh['seq'=16,'ctx'=8] {'seq'}, dimensions={2} | all-to-all | bytes 1048576 | tf_op jit(solution)/shard_map/all_to_all | solution.py:55
  43.8 5.2 %gather_fusion.1 = bf16[384,2,8,128]{3,2,1,0:T(8,128)(2,1)S(1)} fusion(bf16[128,2,8,8,128]{4,3,2,1,0:T(8,128)(2,1)} %param.12, s32[384]{0:T(512)S(1)} %reshape.354), kind=kCustom, calls=%fused_computation.1 | custom fusion | bytes 3148800 | tf_op jit(solution)/shard_map/gather | solution.py:99
  49.0 8.0 %broadcast_in_dim.202 = bf16[16,8,2,12,2,8,128]{6,5,4,3,2,1,0:T(8,128)(2,1)} broadcast(bf16[16,2,12,2,8,128]{5,4,3,2,1,0:T(8,128)(2,1)S(1)} %bitcast.169), dimensions={0,2,3,4,5,6} | broadcast | bytes 14155776 | tf_op jit(solution)/shard_map/broadcast_in_dim | solution.py:101
  57.0 11.0 %all-to-all-start.2 = ((bf16[128,1,2,12,2,8,128]{6,5,4,3,2,1,0:T(8,128)(2,1)}), bf16[128,1,2,12,2,8,128]{6,5,4,3,2,1,0:T(8,128)(2,1)}, u32[]{:S(2)}, u32[]{:S(2)}) async-start(bf16[128,1,2,12,2,8,128]{6,5,4,3,2,1,0:T(8,128)(2,1)} %bitcast.166), calls=%async_computation.2 | async-start | bytes 25165824 | tf_op jit(solution)/shard_map/all_to_all | solution.py:104
  68.2 133.7 %while.41 = (s32[]{:T(128)}, f32[2,1024,1]{1,0,2:T(2,128)S(1)}, f32[2,1024,1]{1,0,2:T(2,128)S(1)}, f32[2,1024,128]{2,1,0:T(8,128)S(1)}, bf16[2,8192,128]{2,1,0:T...) while((s32[]{:T(128)}, f32[2,1024,1]{1,0,2:T(2,128)S(1)}, ...), condition=%wide.region_3.4_spmd.clone.clone, body=%wide.region_0.3_spmd.clone.clone.sunk | while | flops 1102876672 | bytes 32655572 | solution.py:83
  68.9 6.0 %fusion.98 = (f32[2,1024]{1,0:T(2,128)S(1)}, f32[1024,1024,2]{1,0,2:T(8,128)}) fusion(pred[1024,1024]{0,1:T(8,128)(4,1)S(1)} %broadcast_compare_fusion.4, bf16[1024,2,128]{2,0,1:T(8,128)(2,1)S(1)} %get-tuple-element.746, bf16[2,8192,128]{2,1,0:T(8,128)(2,1)} %get-tuple-element.745, s32[]{:T(128)S(6)} %select_n.332), kind=kOutput, calls=%fused_computation.32.clone.1 | convolution fusion | flops 543160320 | bytes 10231812 | tf_op jit(solution)/shard_map/while/body/eval_jaxpr/qpd,kd->pqk/dot_general | solution.py:71
  79.5 5.3 %fusion.101 = f32[2,1024,128]{2,1,0:T(8,128)S(1)} fusion(f32[1024,1024,2]{1,0,2:T(8,128)} %get-tuple-element.715, f32[2,1024]{1,0:T(2,128)S(1)} %bitcast.176, pred[1024,1024]{0,1:T(8,128)(4,1)S(1)} %broadcast_compare_fusion.4, f32[2,1024,128]{2,1,0:T(8,128)S(1)} %get-tuple-element.732, f32[2,1024]{1,0:T(2,128)S(1)} %get-tuple-element.716, ...), kind=kOutput, calls=%fused_computation.38.clone.1 | convolution fusion | flops 548143104 | bytes 11812873 | tf_op jit(solution)/shard_map/while/body/eval_jaxpr/pqk,kd->pqd/dot_general | solution.py:77
  85.6 6.0 %fusion.98 = (f32[2,1024]{1,0:T(2,128)S(1)}, f32[1024,1024,2]{1,0,2:T(8,128)}) fusion(pred[1024,1024]{0,1:T(8,128)(4,1)S(1)} %broadcast_compare_fusion.4, bf16[1024,2,128]{2,0,1:T(8,128)(2,1)S(1)} %get-tuple-element.746, bf16[2,8192,128]{2,1,0:T(8,128)(2,1)} %get-tuple-element.745, s32[]{:T(128)S(6)} %select_n.332), kind=kOutput, calls=%fused_computation.32.clone.1 | convolution fusion | flops 543160320 | bytes 10231812 | tf_op jit(solution)/shard_map/while/body/eval_jaxpr/qpd,kd->pqk/dot_general | solution.py:71
  96.2 5.3 %fusion.101 = f32[2,1024,128]{2,1,0:T(8,128)S(1)} fusion(f32[1024,1024,2]{1,0,2:T(8,128)} %get-tuple-element.715, f32[2,1024]{1,0:T(2,128)S(1)} %bitcast.176, pred[1024,1024]{0,1:T(8,128)(4,1)S(1)} %broadcast_compare_fusion.4, f32[2,1024,128]{2,1,0:T(8,128)S(1)} %get-tuple-element.732, f32[2,1024]{1,0:T(2,128)S(1)} %get-tuple-element.716, ...), kind=kOutput, calls=%fused_computation.38.clone.1 | convolution fusion | flops 548143104 | bytes 11812873 | tf_op jit(solution)/shard_map/while/body/eval_jaxpr/pqk,kd->pqd/dot_general | solution.py:77
  102.3 6.0 %fusion.98 = (f32[2,1024]{1,0:T(2,128)S(1)}, f32[1024,1024,2]{1,0,2:T(8,128)}) fusion(pred[1024,1024]{0,1:T(8,128)(4,1)S(1)} %broadcast_compare_fusion.4, bf16[1024,2,128]{2,0,1:T(8,128)(2,1)S(1)} %get-tuple-element.746, bf16[2,8192,128]{2,1,0:T(8,128)(2,1)} %get-tuple-element.745, s32[]{:T(128)S(6)} %select_n.332), kind=kOutput, calls=%fused_computation.32.clone.1 | convolution fusion | flops 543160320 | bytes 10231812 | tf_op jit(solution)/shard_map/while/body/eval_jaxpr/qpd,kd->pqk/dot_general | solution.py:71
  113.0 5.3 %fusion.101 = f32[2,1024,128]{2,1,0:T(8,128)S(1)} fusion(f32[1024,1024,2]{1,0,2:T(8,128)} %get-tuple-element.715, f32[2,1024]{1,0:T(2,128)S(1)} %bitcast.176, pred[1024,1024]{0,1:T(8,128)(4,1)S(1)} %broadcast_compare_fusion.4, f32[2,1024,128]{2,1,0:T(8,128)S(1)} %get-tuple-element.732, f32[2,1024]{1,0:T(2,128)S(1)} %get-tuple-element.716, ...), kind=kOutput, calls=%fused_computation.38.clone.1 | convolution fusion | flops 548143104 | bytes 11812873 | tf_op jit(solution)/shard_map/while/body/eval_jaxpr/pqk,kd->pqd/dot_general | solution.py:77
  119.0 6.0 %fusion.98 = (f32[2,1024]{1,0:T(2,128)S(1)}, f32[1024,1024,2]{1,0,2:T(8,128)}) fusion(pred[1024,1024]{0,1:T(8,128)(4,1)S(1)} %broadcast_compare_fusion.4, bf16[1024,2,128]{2,0,1:T(8,128)(2,1)S(1)} %get-tuple-element.746, bf16[2,8192,128]{2,1,0:T(8,128)(2,1)} %get-tuple-element.745, s32[]{:T(128)S(6)} %select_n.332), kind=kOutput, calls=%fused_computation.32.clone.1 | convolution fusion | flops 543160320 | bytes 10231812 | tf_op jit(solution)/shard_map/while/body/eval_jaxpr/qpd,kd->pqk/dot_general | solution.py:71
  129.7 5.3 %fusion.101 = f32[2,1024,128]{2,1,0:T(8,128)S(1)} fusion(f32[1024,1024,2]{1,0,2:T(8,128)} %get-tuple-element.715, f32[2,1024]{1,0:T(2,128)S(1)} %bitcast.176, pred[1024,1024]{0,1:T(8,128)(4,1)S(1)} %broadcast_compare_fusion.4, f32[2,1024,128]{2,1,0:T(8,128)S(1)} %get-tuple-element.732, f32[2,1024]{1,0:T(2,128)S(1)} %get-tuple-element.716, ...), kind=kOutput, calls=%fused_computation.38.clone.1 | convolution fusion | flops 548143104 | bytes 11812873 | tf_op jit(solution)/shard_map/while/body/eval_jaxpr/pqk,kd->pqd/dot_general | solution.py:77
  135.8 6.0 %fusion.98 = (f32[2,1024]{1,0:T(2,128)S(1)}, f32[1024,1024,2]{1,0,2:T(8,128)}) fusion(pred[1024,1024]{0,1:T(8,128)(4,1)S(1)} %broadcast_compare_fusion.4, bf16[1024,2,128]{2,0,1:T(8,128)(2,1)S(1)} %get-tuple-element.746, bf16[2,8192,128]{2,1,0:T(8,128)(2,1)} %get-tuple-element.745, s32[]{:T(128)S(6)} %select_n.332), kind=kOutput, calls=%fused_computation.32.clone.1 | convolution fusion | flops 543160320 | bytes 10231812 | tf_op jit(solution)/shard_map/while/body/eval_jaxpr/qpd,kd->pqk/dot_general | solution.py:71
  146.4 5.3 %fusion.101 = f32[2,1024,128]{2,1,0:T(8,128)S(1)} fusion(f32[1024,1024,2]{1,0,2:T(8,128)} %get-tuple-element.715, f32[2,1024]{1,0:T(2,128)S(1)} %bitcast.176, pred[1024,1024]{0,1:T(8,128)(4,1)S(1)} %broadcast_compare_fusion.4, f32[2,1024,128]{2,1,0:T(8,128)S(1)} %get-tuple-element.732, f32[2,1024]{1,0:T(2,128)S(1)} %get-tuple-element.716, ...), kind=kOutput, calls=%fused_computation.38.clone.1 | convolution fusion | flops 548143104 | bytes 11812873 | tf_op jit(solution)/shard_map/while/body/eval_jaxpr/pqk,kd->pqd/dot_general | solution.py:77
  152.5 6.0 %fusion.98 = (f32[2,1024]{1,0:T(2,128)S(1)}, f32[1024,1024,2]{1,0,2:T(8,128)}) fusion(pred[1024,1024]{0,1:T(8,128)(4,1)S(1)} %broadcast_compare_fusion.4, bf16[1024,2,128]{2,0,1:T(8,128)(2,1)S(1)} %get-tuple-element.746, bf16[2,8192,128]{2,1,0:T(8,128)(2,1)} %get-tuple-element.745, s32[]{:T(128)S(6)} %select_n.332), kind=kOutput, calls=%fused_computation.32.clone.1 | convolution fusion | flops 543160320 | bytes 10231812 | tf_op jit(solution)/shard_map/while/body/eval_jaxpr/qpd,kd->pqk/dot_general | solution.py:71
  163.1 5.3 %fusion.101 = f32[2,1024,128]{2,1,0:T(8,128)S(1)} fusion(f32[1024,1024,2]{1,0,2:T(8,128)} %get-tuple-element.715, f32[2,1024]{1,0:T(2,128)S(1)} %bitcast.176, pred[1024,1024]{0,1:T(8,128)(4,1)S(1)} %broadcast_compare_fusion.4, f32[2,1024,128]{2,1,0:T(8,128)S(1)} %get-tuple-element.732, f32[2,1024]{1,0:T(2,128)S(1)} %get-tuple-element.716, ...), kind=kOutput, calls=%fused_computation.38.clone.1 | convolution fusion | flops 548143104 | bytes 11812873 | tf_op jit(solution)/shard_map/while/body/eval_jaxpr/pqk,kd->pqd/dot_general | solution.py:77
  169.2 6.0 %fusion.98 = (f32[2,1024]{1,0:T(2,128)S(1)}, f32[1024,1024,2]{1,0,2:T(8,128)}) fusion(pred[1024,1024]{0,1:T(8,128)(4,1)S(1)} %broadcast_compare_fusion.4, bf16[1024,2,128]{2,0,1:T(8,128)(2,1)S(1)} %get-tuple-element.746, bf16[2,8192,128]{2,1,0:T(8,128)(2,1)} %get-tuple-element.745, s32[]{:T(128)S(6)} %select_n.332), kind=kOutput, calls=%fused_computation.32.clone.1 | convolution fusion | flops 543160320 | bytes 10231812 | tf_op jit(solution)/shard_map/while/body/eval_jaxpr/qpd,kd->pqk/dot_general | solution.py:71
  179.8 5.3 %fusion.101 = f32[2,1024,128]{2,1,0:T(8,128)S(1)} fusion(f32[1024,1024,2]{1,0,2:T(8,128)} %get-tuple-element.715, f32[2,1024]{1,0:T(2,128)S(1)} %bitcast.176, pred[1024,1024]{0,1:T(8,128)(4,1)S(1)} %broadcast_compare_fusion.4, f32[2,1024,128]{2,1,0:T(8,128)S(1)} %get-tuple-element.732, f32[2,1024]{1,0:T(2,128)S(1)} %get-tuple-element.716, ...), kind=kOutput, calls=%fused_computation.38.clone.1 | convolution fusion | flops 548143104 | bytes 11812873 | tf_op jit(solution)/shard_map/while/body/eval_jaxpr/pqk,kd->pqd/dot_general | solution.py:77
  185.9 6.0 %fusion.98 = (f32[2,1024]{1,0:T(2,128)S(1)}, f32[1024,1024,2]{1,0,2:T(8,128)}) fusion(pred[1024,1024]{0,1:T(8,128)(4,1)S(1)} %broadcast_compare_fusion.4, bf16[1024,2,128]{2,0,1:T(8,128)(2,1)S(1)} %get-tuple-element.746, bf16[2,8192,128]{2,1,0:T(8,128)(2,1)} %get-tuple-element.745, s32[]{:T(128)S(6)} %select_n.332), kind=kOutput, calls=%fused_computation.32.clone.1 | convolution fusion | flops 543160320 | bytes 10231812 | tf_op jit(solution)/shard_map/while/body/eval_jaxpr/qpd,kd->pqk/dot_general | solution.py:71
  196.5 5.3 %fusion.101 = f32[2,1024,128]{2,1,0:T(8,128)S(1)} fusion(f32[1024,1024,2]{1,0,2:T(8,128)} %get-tuple-element.715, f32[2,1024]{1,0:T(2,128)S(1)} %bitcast.176, pred[1024,1024]{0,1:T(8,128)(4,1)S(1)} %broadcast_compare_fusion.4, f32[2,1024,128]{2,1,0:T(8,128)S(1)} %get-tuple-element.732, f32[2,1024]{1,0:T(2,128)S(1)} %get-tuple-element.716, ...), kind=kOutput, calls=%fused_computation.38.clone.1 | convolution fusion | flops 548143104 | bytes 11812873 | tf_op jit(solution)/shard_map/while/body/eval_jaxpr/pqk,kd->pqd/dot_general | solution.py:77
  201.9 16.9 %all-to-all-done.2 = bf16[128,1,2,12,2,8,128]{6,5,4,3,2,1,0:T(8,128)(2,1)} async-done(((bf16[128,1,2,12,2,8,128]{6,5,4,3,2,1,0:T(8,128)(2,1)}), bf16[128,1,2,12,2,8,128]{6,5,4,3,2,1,0:T(8,128)(2,1)}, u32[]{:S(2)}, u32[]{:S(2)}) %all-to-all-start.2) | async-done | bytes 12582944 | tf_op jit(solution)/shard_map/all_to_all | solution.py:104
  218.8 11.6 %copy.64 = bf16[2,8,12,2,16,8,128]{6,5,4,3,2,1,0:T(8,128)(2,1)} copy(bf16[2,8,12,2,16,8,128]{6,5,3,2,0,1,4:T(8,128)(2,1)} %bitcast.20) | data formatting | bytes 25165824 | tf_op jit(solution)/shard_map/transpose | solution.py:106
  230.3 105.3 %while.40 = (s32[]{:T(128)}, f32[2,1024,1]{1,0,2:T(2,128)S(1)}, f32[2,1024,1]{1,0,2:T(2,128)S(1)}, f32[2,1024,128]{2,1,0:T(8,128)S(1)}, pred[8,2,12]{2,1,0:T(4,1...) while((s32[]{:T(128)}, f32[2,1024,1]{1,0,2:T(2,128)S(1)}, ...), condition=%wide.region_11.12_spmd, body=%wide.region_8.11_spmd.sunk | while | flops 1652037632 | bytes 45238536 | solution.py:130
  238.3 5.2 %fusion.94 = f32[2,1024,128]{2,1,0:T(8,128)S(1)} fusion(bf16[2,1536,128]{2,1,0:T(8,128)(2,1)S(1)} %bitcast.168, f32[2,1536,1024]{2,1,0:T(8,128)S(1)} %get-tuple-element.701, f32[2,1024]{1,0:T(2,128)S(1)} %bitcast.174, pred[2,1536]{1,0:T(4,128)(4,1)S(1)} %bitcast.172, f32[2,1024,128]{2,1,0:T(8,128)S(1)} %get-tuple-element.768, ...), kind=kOutput, calls=%fused_computation.17.clone.1 | convolution fusion | flops 821559296 | bytes 15485952 | tf_op jit(solution)/shard_map/while/body/eval_jaxpr/pqk,pkd->pqd/dot_general | solution.py:124
  251.5 5.2 %fusion.94 = f32[2,1024,128]{2,1,0:T(8,128)S(1)} fusion(bf16[2,1536,128]{2,1,0:T(8,128)(2,1)S(1)} %bitcast.168, f32[2,1536,1024]{2,1,0:T(8,128)S(1)} %get-tuple-element.701, f32[2,1024]{1,0:T(2,128)S(1)} %bitcast.174, pred[2,1536]{1,0:T(4,128)(4,1)S(1)} %bitcast.172, f32[2,1024,128]{2,1,0:T(8,128)S(1)} %get-tuple-element.768, ...), kind=kOutput, calls=%fused_computation.17.clone.1 | convolution fusion | flops 821559296 | bytes 15485952 | tf_op jit(solution)/shard_map/while/body/eval_jaxpr/pqk,pkd->pqd/dot_general | solution.py:124
  264.7 5.2 %fusion.94 = f32[2,1024,128]{2,1,0:T(8,128)S(1)} fusion(bf16[2,1536,128]{2,1,0:T(8,128)(2,1)S(1)} %bitcast.168, f32[2,1536,1024]{2,1,0:T(8,128)S(1)} %get-tuple-element.701, f32[2,1024]{1,0:T(2,128)S(1)} %bitcast.174, pred[2,1536]{1,0:T(4,128)(4,1)S(1)} %bitcast.172, f32[2,1024,128]{2,1,0:T(8,128)S(1)} %get-tuple-element.768, ...), kind=kOutput, calls=%fused_computation.17.clone.1 | convolution fusion | flops 821559296 | bytes 15485952 | tf_op jit(solution)/shard_map/while/body/eval_jaxpr/pqk,pkd->pqd/dot_general | solution.py:124
  277.8 5.2 %fusion.94 = f32[2,1024,128]{2,1,0:T(8,128)S(1)} fusion(bf16[2,1536,128]{2,1,0:T(8,128)(2,1)S(1)} %bitcast.168, f32[2,1536,1024]{2,1,0:T(8,128)S(1)} %get-tuple-element.701, f32[2,1024]{1,0:T(2,128)S(1)} %bitcast.174, pred[2,1536]{1,0:T(4,128)(4,1)S(1)} %bitcast.172, f32[2,1024,128]{2,1,0:T(8,128)S(1)} %get-tuple-element.768, ...), kind=kOutput, calls=%fused_computation.17.clone.1 | convolution fusion | flops 821559296 | bytes 15485952 | tf_op jit(solution)/shard_map/while/body/eval_jaxpr/pqk,pkd->pqd/dot_general | solution.py:124
  291.0 5.2 %fusion.94 = f32[2,1024,128]{2,1,0:T(8,128)S(1)} fusion(bf16[2,1536,128]{2,1,0:T(8,128)(2,1)S(1)} %bitcast.168, f32[2,1536,1024]{2,1,0:T(8,128)S(1)} %get-tuple-element.701, f32[2,1024]{1,0:T(2,128)S(1)} %bitcast.174, pred[2,1536]{1,0:T(4,128)(4,1)S(1)} %bitcast.172, f32[2,1024,128]{2,1,0:T(8,128)S(1)} %get-tuple-element.768, ...), kind=kOutput, calls=%fused_computation.17.clone.1 | convolution fusion | flops 821559296 | bytes 15485952 | tf_op jit(solution)/shard_map/while/body/eval_jaxpr/pqk,pkd->pqd/dot_general | solution.py:124
  304.2 5.2 %fusion.94 = f32[2,1024,128]{2,1,0:T(8,128)S(1)} fusion(bf16[2,1536,128]{2,1,0:T(8,128)(2,1)S(1)} %bitcast.168, f32[2,1536,1024]{2,1,0:T(8,128)S(1)} %get-tuple-element.701, f32[2,1024]{1,0:T(2,128)S(1)} %bitcast.174, pred[2,1536]{1,0:T(4,128)(4,1)S(1)} %bitcast.172, f32[2,1024,128]{2,1,0:T(8,128)S(1)} %get-tuple-element.768, ...), kind=kOutput, calls=%fused_computation.17.clone.1 | convolution fusion | flops 821559296 | bytes 15485952 | tf_op jit(solution)/shard_map/while/body/eval_jaxpr/pqk,pkd->pqd/dot_general | solution.py:124
  317.4 5.2 %fusion.94 = f32[2,1024,128]{2,1,0:T(8,128)S(1)} fusion(bf16[2,1536,128]{2,1,0:T(8,128)(2,1)S(1)} %bitcast.168, f32[2,1536,1024]{2,1,0:T(8,128)S(1)} %get-tuple-element.701, f32[2,1024]{1,0:T(2,128)S(1)} %bitcast.174, pred[2,1536]{1,0:T(4,128)(4,1)S(1)} %bitcast.172, f32[2,1024,128]{2,1,0:T(8,128)S(1)} %get-tuple-element.768, ...), kind=kOutput, calls=%fused_computation.17.clone.1 | convolution fusion | flops 821559296 | bytes 15485952 | tf_op jit(solution)/shard_map/while/body/eval_jaxpr/pqk,pkd->pqd/dot_general | solution.py:124
  336.9 19.0 %all_to_all.55 = bf16[16,64,256]{2,1,0:T(8,128)(2,1)S(1)} all-to-all(bf16[16,64,256]{2,1,0:T(8,128)(2,1)S(1)} %reshape.344), channel_id=1, replica_groups=mesh['seq'=16,'ctx'=8] {'seq'}, dimensions={0} | all-to-all | bytes 1048576 | tf_op jit(solution)/shard_map/all_to_all | solution.py:134
  (174 shorter events, 131.6 us)
Async XLA Ops:
  6.5 1.0 copy-start
  6.5 28.3 %copy-start.2 = (s32[1024]{0:T(1024)S(1)}, s32[1024]{0:T(1024)}, u32[]{:S(2)}) copy-start(s32[1024]{0:T(1024)} %param.15) | copy-start | bytes 12292
  6.5 61.6 %all-gather.2.cloned.1.call-start = ((), (), s32[]{:S(2)}) async-start(), calls=%async_computation.4 | async-start | bytes 4718592 | tf_op jit(solution)/shard_map/all_gather | solution.py:65
  29.7 19.3 %all-to-all-start.1 = ((bf16[64,16,256]{2,0,1:T(8,128)(2,1)}), bf16[64,16,256]{2,0,1:T(8,128)(2,1)S(1)}, u32[]{:S(2)}, u32[]{:S(2)}) async-start(bf16[64,16,256]{2,0,1:T(8,128)(2,1)} %bitcast.118), calls=%async_computation.1 | async-start | bytes 1048576 | tf_op jit(solution)/shard_map/all_to_all | solution.py:51
  57.0 161.8 %all-to-all-start.2 = ((bf16[128,1,2,12,2,8,128]{6,5,4,3,2,1,0:T(8,128)(2,1)}), bf16[128,1,2,12,2,8,128]{6,5,4,3,2,1,0:T(8,128)(2,1)}, u32[]{:S(2)}, u32[]{:S(2)}) async-start(bf16[128,1,2,12,2,8,128]{6,5,4,3,2,1,0:T(8,128)(2,1)} %bitcast.166), calls=%async_computation.2 | async-start | bytes 25165824 | tf_op jit(solution)/shard_map/all_to_all | solution.py:104
  335.7 21.1 %copy-start.1 = (bf16[2,64,1024]{2,1,0:T(8,128)(2,1)S(1)}, bf16[2,64,1024]{2,1,0:T(8,128)(2,1)}, u32[]{:S(2)}) copy-start(bf16[2,64,1024]{2,1,0:T(8,128)(2,1)} %param.11) | copy-start | bytes 786436
Sparse Core Ops, SparseCore 0:
  27.9 29.7 all-gather.1
where the time goes:
time: 367 us; the launch traced here: 364 us
  matrix products  154 us (42%)
  other arithmetic  76.5 us (21%)
  local copies, waits for them, and re-layouts  48.3 us (13%)
  blocking collectives  38.3 us (10%)
  waiting for transfers between devices  16.9 us (5%)
  starting transfers between devices  14.6 us (4%)
  between operations  13.6 us (4%)
    reduce_sum x16, other arithmetic, online_update(): new_sum = running_sum * fading + jnp.sum(weights, axis=2, keepdims=True)  64.7 us
    dot_general x8, matrix products, visit(): jnp.einsum('qpd,kd->pqk', own_queries, shard_kv[0], preferred_element_typ...  47.7 us
    dot_general x8, matrix products, stretch_mix(): jnp.einsum('pqk,kd->pqd', rounded, shard_kv[1], preferred_element_type=jn...  42.8 us
    dot_general x8, matrix products, block_mix(): jnp.einsum('pqk,pkd->pqd', rounded, block_values, preferred_element_type=...  41.2 us
    dot_general x8, matrix products, visit(): jnp.einsum('qpd,pkd->pqk', own_queries, block_keys, preferred_element_typ...  22.7 us
    all_to_all x1, blocking collectives, on_device(): lax.all_to_all(widened_kv, 'seq', split_axis=2, concat_axis=1, tiled=True)  19.3 us
    all_to_all x1, blocking collectives, on_device(): lax.all_to_all(outgoing, 'seq', split_axis=0, concat_axis=2, tiled=True)  19 us
    all_to_all x1, waiting for transfers between devices, on_device(): lax.all_to_all(widened, ('seq', 'ctx'), split_axis=0, concat_axis=1, tile...  16.9 us
  transfers between devices with their start and end apart: 3, of which 1 were waited for; matrix products, arithmetic and copies ran while one was open for 44% of the time, Pallas kernels for 0%

commit v1 on v0

v1 whole, which is shorter than its diff:
```python
import jax
import jax.numpy as jnp
from jax import lax
from jax.experimental import pallas as pl
from jax.experimental.pallas import tpu as pltpu
from jax.sharding import PartitionSpec as P

H = 32
KVH = 8
HD = 128
BLK = 128
NSEL = 32
CAP = 12
GROUP = H // KVH
TOK = 64
STRETCH = 8192
LOG2E = 1.4426950408889634
EXP_SCALE = HD**-0.5 * LOG2E
masked_value = -1e30
Q_TILE = 256
K_TILE = 1024
CACHED = NSEL * BLK


def flash_kernel(q_ref, kv_ref, ckv_ref, out_ref):
    tile = pl.program_id(0)
    quarter = lax.rem(lax.axis_index("seq"), 4)
    q = q_ref[...]
    ones = jnp.ones((K_TILE, HD), jnp.bfloat16)

    def step(carry, keys, values, masked):
        peak, acc = carry
        scores = lax.dot_general(q, keys, (((1,), (1,)), ((), ())), preferred_element_type=jnp.float32)
        if masked:
            row = lax.broadcasted_iota(jnp.int32, scores.shape, 0)
            col = lax.broadcasted_iota(jnp.int32, scores.shape, 1)
            limit = row // 128 * 512 + quarter * 128 + row % 128
            scores = jnp.where(col <= limit, scores, masked_value)
        new_peak = jnp.maximum(peak, jnp.max(scores, axis=1, keepdims=True))
        weights = jnp.exp2((scores - new_peak) * EXP_SCALE)
        fading = jnp.exp2((peak - new_peak) * EXP_SCALE)
        mixed = jnp.dot(
            weights.astype(jnp.bfloat16),
            jnp.concatenate([values, ones], axis=1),
            preferred_element_type=jnp.float32,
        )
        return new_peak, acc * fading + mixed

    carry = (
        jnp.full((Q_TILE, 1), masked_value, jnp.float32),
        jnp.zeros((Q_TILE, 2 * HD), jnp.float32),
    )
    for block in range(CACHED // K_TILE):
        rows = pl.ds(block * K_TILE, K_TILE)
        carry = step(carry, ckv_ref[0, rows, :], ckv_ref[1, rows, :], False)

    def full(block, carry):
        rows = pl.ds(pl.multiple_of(block * K_TILE, K_TILE), K_TILE)
        return step(carry, kv_ref[0, rows, :], kv_ref[1, rows, :], False)

    carry = lax.fori_loop(0, tile, full, carry)
    rows = pl.ds(pl.multiple_of(tile * K_TILE, K_TILE), K_TILE)
    peak, acc = step(carry, kv_ref[0, rows, :], kv_ref[1, rows, :], True)
    out_ref[...] = (acc[:, :HD] / acc[:, HD:]).astype(jnp.bfloat16)


def flash(q, kv, ckv):
    return pl.pallas_call(
        flash_kernel,
        grid=(q.shape[0] // Q_TILE,),
        in_specs=[
            pl.BlockSpec((Q_TILE, HD), lambda i: (i, 0)),
            pl.BlockSpec(kv.shape, lambda i: (0, 0, 0), pipeline_mode=pl.Buffered(1)),
            pl.BlockSpec(ckv.shape, lambda i: (0, 0, 0), pipeline_mode=pl.Buffered(1)),
        ],
        out_specs=pl.BlockSpec((Q_TILE, HD), lambda i: (i, 0)),
        out_shape=jax.ShapeDtypeStruct(q.shape, jnp.bfloat16),
        compiler_params=pltpu.CompilerParams(vmem_limit_bytes=48 << 20),
    )(q, kv, ckv)


def block_places(vertical, slash, owner_map, ctx_index):
    nblk = owner_map.shape[0]
    selected = jnp.concatenate([vertical, nblk - 1 - slash], axis=1)
    hit = selected[:, :, None] == jnp.arange(nblk, dtype=jnp.int32)
    storage = jnp.sum(jnp.where(hit, owner_map, 0), axis=2)
    per_ctx = nblk // 8
    owner = storage // per_ctx
    local_row = storage % per_ctx
    order = jnp.arange(NSEL, dtype=jnp.int32)
    earlier = (owner[:, :, None] == owner[:, None, :]) & (order[None, None, :] < order[None, :, None])
    rank = jnp.sum(earlier.astype(jnp.int32), axis=2)
    slot_hit = (owner[:, :, None] == ctx_index) & (rank[:, :, None] == jnp.arange(CAP, dtype=jnp.int32))
    send_rows = jnp.sum(jnp.where(slot_hit, local_row[:, :, None], 0), axis=1)
    in_group = jnp.arange(H, dtype=jnp.int32)[:, None] % GROUP
    places = (owner * GROUP + in_group) * CAP + rank
    return send_rows, places


def on_device(queries, stretch_kv, cache_kv, vertical, slash, owner_map):
    ctx_index = lax.axis_index("ctx")
    send_rows, places = block_places(vertical, slash, owner_map, ctx_index)
    own_places = lax.dynamic_slice_in_dim(places, ctx_index * GROUP, GROUP, 0)
    group_of = jnp.arange(H, dtype=jnp.int32)[:, None] // GROUP
    columns = [[z * 4 + x for z in range(4)] for x in range(4)]
    rows = [[z * 4 + x for x in range(4)] for z in range(4)]

    own_kv = lax.all_to_all(stretch_kv.reshape(2, TOK, KVH, HD), "ctx", split_axis=2, concat_axis=1, tiled=True)
    own_kv = own_kv.reshape(2, 8 * TOK, HD)
    kv = lax.all_gather(own_kv, "seq", axis=1, tiled=True)
    packed = cache_kv[send_rows, :, group_of]
    packed = packed.reshape(KVH, GROUP * CAP, 2, 8, HD)
    received = lax.all_to_all(packed, "ctx", split_axis=0, concat_axis=0, tiled=True)
    compact = received.reshape(KVH * GROUP * CAP, 2, 8, HD)[own_places]
    compact = jnp.transpose(compact, (0, 2, 1, 3, 4))
    by_head = lax.all_to_all(compact, "seq", split_axis=0, concat_axis=0, tiled=True, axis_index_groups=columns)
    by_head = by_head.reshape(4, 2, NSEL * 8, HD)
    by_head = jnp.transpose(by_head, (1, 0, 2, 3)).reshape(2, 4 * NSEL * 8, HD)
    ckv = lax.all_gather(by_head, "seq", axis=1, tiled=True, axis_index_groups=rows)

    q = lax.all_to_all(queries.reshape(TOK, KVH, GROUP * HD), "ctx", split_axis=1, concat_axis=0, tiled=True)
    q = q.reshape(4, 2 * TOK, GROUP, HD)
    q = jnp.transpose(q, (2, 0, 1, 3)).reshape(16, 2 * TOK, HD)
    q = lax.all_to_all(q, "seq", split_axis=0, concat_axis=0, tiled=True)
    out = flash(q.reshape(16 * 2 * TOK, HD), kv, ckv)
    out = lax.all_to_all(out.reshape(16, 2 * TOK, HD), "seq", split_axis=0, concat_axis=0, tiled=True)
    out = jnp.transpose(out.reshape(GROUP, 8 * TOK, HD), (1, 0, 2)).reshape(8 * TOK, 1, GROUP * HD)
    out = lax.all_to_all(out, "ctx", split_axis=0, concat_axis=1, tiled=True)
    return out.reshape(TOK, H * HD)


def solution(mesh):
    placed = (
        P(("seq", "ctx"), None),
        P(None, ("seq", "ctx"), None),
        P("ctx", None, None, "seq", None),
        P(),
        P(),
        P(),
    )
    return jax.shard_map(
        on_device, mesh=mesh, in_specs=placed, out_specs=P(("seq", "ctx"), None), check_vma=False
    )
```

time: 367 us -> 233 us (0.63)
  matrix products: 154 us -> 0 us
  other arithmetic: 76.5 us -> 5.22 us
  Pallas kernels: 0 us -> 47.1 us
  waiting for transfers between devices: 16.9 us -> 63.8 us
  blocking collectives: 38.3 us -> 84.2 us
  local copies, waits for them, and re-layouts: 48.3 us -> 13.7 us
  starting transfers between devices: 14.6 us -> 4.76 us
    dot_general x32 -> x0, matrix products: 154 us -> none  [the longest x8 47.7 us: visit(): jnp.einsum('qpd,kd->pqk', own_queries, shard_kv[0], preferred_element_typ...]
    reduce_sum x17 -> x3, other arithmetic: 65 us -> 2.61 us  [the longest x1 1.55 us: block_places(): storage = jnp.sum(jnp.where(hit, owner_map, 0), axis=2)]
    pallas_call x0 -> x1, Pallas kernels: none -> 47.1 us  [flash(): pl.pallas_call(flash_kernel, grid=(q.shape[0] // Q_TILE,), in_specs=[pl.B...]
    all_to_all x2 -> x6, blocking collectives: 38.3 us -> 84.2 us  [the longest x1 16.6 us: on_device(): lax.all_to_all(out.reshape(16, 2 * TOK, HD), 'seq', split_axis=0, concat_...]
    all_gather x1 -> x2, waiting for transfers between devices: 0.02 us -> 42.5 us  [the longest x1 42.5 us: on_device(): kv = lax.all_gather(own_kv, 'seq', axis=1, tiled=True)]
    slice x8 -> x0, local copies, waits for them, and re-layouts: 11.9 us -> none  [visit(): block_values = blocks[:, :, 1].reshape(per_device, CAP * BLK, HD)]
    transpose x2 -> x3, local copies, waits for them, and re-layouts: 12.1 us -> 0.4 us  [the longest x1 0.21 us: on_device(): jnp.transpose(out.reshape(GROUP, 8 * TOK, HD), (1, 0, 2))]
    all_to_all x2 -> x1, starting transfers between devices: 14.5 us -> 4.69 us  [on_device(): lax.all_to_all(packed, 'ctx', split_axis=0, concat_axis=0, tiled=True)]
  transfers between devices with their start and end apart: 3 -> 3, of which waited for: 1 -> 2; matrix products, arithmetic and copies ran while one was open for 44% -> 1% of each run, Pallas kernels for 0% -> 0%
where the time goes in v1:
time: 233 us; the launch traced here: 232 us
  blocking collectives  84.2 us (36%)
  waiting for transfers between devices  63.8 us (27%)
  Pallas kernels  47.1 us (20%)
  local copies, waits for them, and re-layouts  13.7 us (6%)
  between operations  13.6 us (6%)
  other arithmetic  5.22 us (2%)
  starting transfers between devices  4.76 us (2%)
    pallas_call x1, Pallas kernels, flash(): pl.pallas_call(flash_kernel, grid=(q.shape[0] // Q_TILE,), in_specs=[pl.B...  47.1 us
    all_gather x1, waiting for transfers between devices, on_device(): kv = lax.all_gather(own_kv, 'seq', axis=1, tiled=True)  42.5 us
    all_to_all x1, waiting for transfers between devices, on_device(): lax.all_to_all(packed, 'ctx', split_axis=0, concat_axis=0, tiled=True)  21.3 us
    all_to_all x1, blocking collectives, on_device(): lax.all_to_all(out.reshape(16, 2 * TOK, HD), 'seq', split_axis=0, concat_...  16.6 us
    all_to_all x1, blocking collectives, on_device(): q = lax.all_to_all(q, 'seq', split_axis=0, concat_axis=0, tiled=True)  16 us
    all_to_all x1, blocking collectives, on_device(): out = lax.all_to_all(out, 'ctx', split_axis=0, concat_axis=1, tiled=True)  14.5 us
    all_to_all x1, blocking collectives, on_device(): lax.all_to_all(compact, 'seq', split_axis=0, concat_axis=0, tiled=True, a...  14.4 us
    all_to_all x1, blocking collectives, on_device(): lax.all_to_all(queries.reshape(TOK, KVH, GROUP * HD), 'ctx', split_axis=1...  12.8 us
  transfers between devices with their start and end apart: 3, of which 2 were waited for; matrix products, arithmetic and copies ran while one was open for 1% of the time, Pallas kernels for 0%

profile of v1, /device:TPU:0, one launch (start us, length us, event | category | flops | bytes accessed | tf_op | source)
XLA Modules:
  0.0 232.3 jit_solution(11632018092592282037)
XLA Ops:
  6.5 0.8 broadcast_subtract_fusion
  7.3 0.7 pad_add_fusion
  8.1 1.6 select_reduce_fusion
  9.7 0.8 convert_reduce_fusion
  10.5 0.3 select_reduce_fusion.1
  10.8 0.1 reshape.201
  11.0 6.2 %gather_fusion = bf16[384,2,8,128]{3,2,1,0:T(8,128)(2,1)} fusion(bf16[128,2,8,8,128]{4,3,2,1,0:T(8,128)(2,1)} %param.8, s32[384]{0:T(512)S(1)} %reshape.201), kind=kCustom, calls=%fused_computation | custom fusion | bytes 3148800 | tf_op jit(solution)/shard_map/gather | solution.py:111
  17.1 4.7 %all-to-all-start.3 = ((bf16[8,48,2,8,128]{4,3,2,1,0:T(8,128)(2,1)}), bf16[8,48,2,8,128]{4,3,2,1,0:T(8,128)(2,1)S(1)}, u32[]{:S(2)}, u32[]{:S(2)}) async-start(bf16[8,48,2,8,128]{4,3,2,1,0:T(8,128)(2,1)} %bitcast.9), calls=%async_computation.3 | async-start | bytes 3145728 | tf_op jit(solution)/shard_map/all_to_all | solution.py:113
  22.1 21.3 %all-to-all-done.3 = bf16[8,48,2,8,128]{4,3,2,1,0:T(8,128)(2,1)S(1)} async-done(((bf16[8,48,2,8,128]{4,3,2,1,0:T(8,128)(2,1)}), bf16[8,48,2,8,128]{4,3,2,1,0:T(8,128)(2,1)S(1)}, u32[]{:S(2)}, u32[]{:S(2)}) %all-to-all-start.3) | async-done | bytes 1572896 | tf_op jit(solution)/shard_map/all_to_all | solution.py:113
  43.4 0.7 gather_fusion.1
  44.1 0.1 copy.51
  44.2 14.4 %all_to_all.65 = bf16[4,2,32,8,128]{4,3,2,1,0:T(8,128)(2,1)S(1)} all-to-all(bf16[4,2,32,8,128]{4,3,2,1,0:T(8,128)(2,1)S(1)} %copy.51), channel_id=1, replica_groups={{0,32,64,96},{8,40,72,104},{16,48,80,112},{24,56,88,120},{1,33,65,97},{..., dimensions={0} | all-to-all | bytes 1048576 | tf_op jit(solution)/shard_map/all_to_all | solution.py:116
  58.6 0.8 copy.52
  59.6 9.9 %all_to_all.66 = bf16[2,64,8,128]{3,1,0,2:T(8,128)(2,1)S(1)} all-to-all(bf16[2,64,8,128]{3,1,0,2:T(8,128)(2,1)S(1)} %copy_bitcast_fusion.1), channel_id=1, replica_groups=mesh['seq'=16,'ctx'=8] {'ctx'}, dimensions={2} | all-to-all | bytes 524288 | tf_op jit(solution)/shard_map/all_to_all | solution.py:108
  69.5 0.7 copy.48
  70.3 12.8 %all_to_all.67 = bf16[64,8,512]{2,0,1:T(8,128)(2,1)S(1)} all-to-all(bf16[64,8,512]{2,0,1:T(8,128)(2,1)S(1)} %bitcast.62), channel_id=1, replica_groups=mesh['seq'=16,'ctx'=8] {'ctx'}, dimensions={1} | all-to-all | bytes 1048576 | tf_op jit(solution)/shard_map/all_to_all | solution.py:121
  83.1 0.1 reshape.188
  83.3 0.1 copy.46
  83.4 16.0 %all_to_all.68 = bf16[16,128,128]{2,1,0:T(8,128)(2,1)S(1)} all-to-all(bf16[16,128,128]{2,1,0:T(8,128)(2,1)S(1)} %bitcast.60), channel_id=1, replica_groups=mesh['seq'=16,'ctx'=8] {'seq'}, dimensions={0} | all-to-all | bytes 1048576 | tf_op jit(solution)/shard_map/all_to_all | solution.py:124
  99.4 42.5 %all-gather.3.cloned.1.call-done.kv_ref = bf16[2,8192,128]{2,1,0:T(8,128)(2,1)} async-done(((bf16[2,512,128]{2,1,0:T(8,128)(2,1)}), bf16[2,8192,128]{2,1,0:T(8,128)(2,1)}) %all-gather.3.cloned.1.call-update) | async-done | bytes 4194320 | tf_op jit(solution)/shard_map/all_gather | solution.py:110
  141.8 1.6 copy-done.1
  143.4 47.1 %shard_map.64 = bf16[2048,128]{1,0:T(8,128)(2,1)S(1)} custom-call(bf16[2048,128]{1,0:T(8,128)(2,1)S(1)} %bitcast.50, bf16[2,8192,128]{2,1,0:T(8,128)(2,1)} %all-gather.3.cloned.1.call-done.kv_ref, bf16[2,4096,128]{2,1,0:T(8,128)(2,1)S(1)} %copy-done.1), custom_call_target="tpu_custom_call" | custom-call | tf_op jit(solution)/shard_map/pallas_call | solution.py:68
  190.5 16.6 %all_to_all.69 = bf16[16,128,128]{2,1,0:T(8,128)(2,1)S(1)} all-to-all(bf16[16,128,128]{2,1,0:T(8,128)(2,1)S(1)} %bitcast.51), channel_id=1, replica_groups=mesh['seq'=16,'ctx'=8] {'seq'}, dimensions={0} | all-to-all | bytes 1048576 | tf_op jit(solution)/shard_map/all_to_all | solution.py:126
  207.1 0.2 copy.53
  207.3 0.5 broadcast.234
  207.9 1.0 reduce
  208.9 0.2 copy.64
  209.1 0.4 reshape.218
  209.5 14.5 %all_to_all.70 = bf16[8,2,16384]{2,1,0:T(2,128)(2,1)S(1)} all-to-all(bf16[8,2,16384]{2,1,0:T(2,128)(2,1)S(1)} %reshape.218), channel_id=1, replica_groups=mesh['seq'=16,'ctx'=8] {'ctx'}, dimensions={0} | all-to-all | bytes 1048576 | tf_op jit(solution)/shard_map/all_to_all | solution.py:128
  224.0 0.5 reshape.219
  224.5 0.1 copy.56
  224.6 0.8 copy.59
  (22 shorter events, 0.7 us)
Async XLA Ops:
  6.5 53.0 %copy-start = (bf16[2,64,1024]{2,1,0:T(8,128)(2,1)S(1)}, bf16[2,64,1024]{2,1,0:T(8,128)(2,1)}, u32[]{:S(2)}) copy-start(bf16[2,64,1024]{2,1,0:T(8,128)(2,1)} %param.7) | copy-start | bytes 786436
  17.1 53.2 %copy-start.2 = (bf16[64,4096]{1,0:T(8,128)(2,1)S(1)}, bf16[64,4096]{1,0:T(8,128)(2,1)}, u32[]{:S(2)}) copy-start(bf16[64,4096]{1,0:T(8,128)(2,1)} %param.6) | copy-start | bytes 1572868
  17.1 26.3 %all-to-all-start.3 = ((bf16[8,48,2,8,128]{4,3,2,1,0:T(8,128)(2,1)}), bf16[8,48,2,8,128]{4,3,2,1,0:T(8,128)(2,1)S(1)}, u32[]{:S(2)}, u32[]{:S(2)}) async-start(bf16[8,48,2,8,128]{4,3,2,1,0:T(8,128)(2,1)} %bitcast.9), calls=%async_computation.3 | async-start | bytes 3145728 | tf_op jit(solution)/shard_map/all_to_all | solution.py:113
  21.8 77.5 %all-gather.5.cloned.1.call-start = ((), (), s32[]{:S(2)}) async-start(), calls=%async_computation.8 | async-start | bytes 2621440 | tf_op jit(solution)/shard_map/all_gather | solution.py:119
  59.5 82.4 %all-gather.3.cloned.1.call-start = ((), (), s32[]{:S(2)}) async-start(), calls=%async_computation.7 | async-start | bytes 4456448 | tf_op jit(solution)/shard_map/all_gather | solution.py:110
  141.8 1.6 copy-start.1
Sparse Core Ops, SparseCore 0:
  59.6 28.2 all-gather.4
  90.0 51.7 all-gather.2

commit v2 on v1

v2 whole, which is shorter than its diff:
```python
import jax
import jax.numpy as jnp
from jax import lax
from jax.experimental import pallas as pl
from jax.experimental.pallas import tpu as pltpu
from jax.sharding import PartitionSpec as P

H = 32
KVH = 8
HD = 128
BLK = 128
NSEL = 32
CAP = 12
GROUP = H // KVH
TOK = 64
STRETCH = 8192
LOG2E = 1.4426950408889634
EXP_SCALE = HD**-0.5 * LOG2E
masked_value = -1e30
Q_TILE = 256
K_TILE = 1024
CACHED = NSEL * BLK


MESH = pl.DeviceIdType.MESH


def remote(src, dst, send_sem, recv_sem, seq, ctx):
    return pltpu.make_async_remote_copy(
        src_ref=src, dst_ref=dst, send_sem=send_sem, recv_sem=recv_sem, device_id=(seq, ctx), device_id_type=MESH
    )


def comm_kernel(
    rows_ref, places_ref, queries, stretch, cache, q_out, kv_out, ckv_out,
    cache_v, packed, arrived, compact, q_mid,
    kv_send, kv_recv, q_send, q_recv, c_send, c_recv, qb_send, qb_recv,
    p1_send, p1_recv, p2_send, p2_recv, cz_send, cz_recv, cx_send, cx_recv, local_sem,
):
    seq, ctx = lax.axis_index("seq"), lax.axis_index("ctx")
    z, x = seq // 4, seq % 4

    def along(axis, delta):
        if axis == "x":
            return z * 4 + (x + delta + 4) % 4
        return (z + delta + 4) % 4 * 4 + x

    barrier = pltpu.get_barrier_semaphore()
    for d in range(1, 8):
        pl.semaphore_signal(barrier, inc=1, device_id=(seq, (ctx + d) % 8), device_id_type=MESH)
    for d in range(1, 16):
        pl.semaphore_signal(barrier, inc=1, device_id=((seq + d) % 16, ctx), device_id_type=MESH)
    load_cache = pltpu.make_async_copy(cache, cache_v, local_sem.at[0])
    load_cache.start()
    pl.semaphore_wait(barrier, 22)

    def lane(index, size):
        return pl.ds(pl.multiple_of(index * size, size), size)

    def kv_a(d, from_ctx, to_ctx):
        return (
            stretch.at[:, :, lane(to_ctx, HD)],
            kv_out.at[:, pl.ds(pl.multiple_of(seq * 512 + from_ctx * TOK, TOK), TOK), :],
        )

    def q_a(d, from_ctx, to_ctx):
        return queries.at[:, lane(to_ctx, GROUP * HD)], q_mid.at[lane(from_ctx, TOK), :]

    sends = []
    for d in range(1, 8):
        peer = (ctx + d) % 8
        sends.append(remote(*kv_a(d, ctx, peer), kv_send.at[d], kv_recv.at[d], seq, peer))
        sends[-1].start()
    own_kv = pltpu.make_async_copy(*kv_a(0, ctx, ctx), local_sem.at[1])
    own_kv.start()
    for d in range(1, 8):
        peer = (ctx + d) % 8
        sends.append(remote(*q_a(d, ctx, peer), q_send.at[d], q_recv.at[d], seq, peer))
        sends[-1].start()
    own_q = pltpu.make_async_copy(*q_a(0, ctx, ctx), local_sem.at[2])
    own_q.start()

    load_cache.wait()
    for d in range(8):
        peer = (ctx + d) % 8

        def pack(member, carry, peer=peer):
            base = (peer * GROUP + member) * CAP
            for slot in range(CAP):
                packed[base + slot] = cache_v[rows_ref[base + slot], :, peer]
            return carry

        lax.fori_loop(0, GROUP, pack, 0)
        if d:
            sends.append(
                remote(
                    packed.at[pl.ds(peer * GROUP * CAP, GROUP * CAP)],
                    arrived.at[pl.ds(ctx * GROUP * CAP, GROUP * CAP)],
                    c_send.at[d], c_recv.at[d], seq, peer,
                )
            )
            sends[-1].start()
        else:
            own_c = pltpu.make_async_copy(
                packed.at[pl.ds(peer * GROUP * CAP, GROUP * CAP)],
                arrived.at[pl.ds(ctx * GROUP * CAP, GROUP * CAP)],
                local_sem.at[3],
            )
            own_c.start()

    own_kv.wait()
    for d in range(1, 8):
        origin = (ctx - d + 8) % 8
        remote(*kv_a(d, origin, ctx), kv_send.at[d], kv_recv.at[d], seq, origin).wait_recv()

    axes = (("x", "z"), ("z", "x"))
    OFFSETS = (0, -1, 1, 2)

    def kv_block(i, s, half=None):
        if half is None:
            return kv_out.at[i, pl.ds(pl.multiple_of(s * 512, 512), 512), :]
        return kv_out.at[i, pl.ds(pl.multiple_of(s * 512 + half * 256, 256), 256), :]

    def at(i, first, second):
        dx, dz = (first, second) if i == 0 else (second, first)
        return (z + dz + 4) % 4 * 4 + (x + dx + 4) % 4

    def first_hop(i, j):
        step = (1, -1, 1, -1)[j]
        block = (0, 0, -1, 1)[j]
        half = (None, None, 0, 1)[j]
        return step, block, half

    def p1(i, j):
        step, block, half = first_hop(i, j)
        ref = kv_block(i, at(i, block, 0), half)
        return remote(ref, ref, p1_send.at[i, j], p1_recv.at[i, j], along(axes[i][0], step), ctx)

    def p1_in(i, j):
        step, block, half = first_hop(i, j)
        ref = kv_block(i, at(i, block - step, 0), half)
        return remote(ref, ref, p1_send.at[i, j], p1_recv.at[i, j], along(axes[i][0], step), ctx)

    def p2(i, p, j):
        step, block, half = first_hop(i, j)
        ref = kv_block(i, at(i, OFFSETS[p], block), half)
        return remote(ref, ref, p2_send.at[i, p, j], p2_recv.at[i, p, j], along(axes[i][1], step), ctx)

    def p2_in(i, p, j):
        step, block, half = first_hop(i, j)
        ref = kv_block(i, at(i, OFFSETS[p], block - step), half)
        return remote(ref, ref, p2_send.at[i, p, j], p2_recv.at[i, p, j], along(axes[i][1], step), ctx)

    def go(copy):
        copy.start()
        sends.append(copy)

    for i in range(2):
        go(p1(i, 0))
        go(p1(i, 1))
    for i in range(2):
        go(p2(i, 0, 0))
        go(p2(i, 0, 1))

    own_q.wait()
    for d in range(1, 8):
        origin = (ctx - d + 8) % 8
        remote(*q_a(d, origin, ctx), q_send.at[d], q_recv.at[d], seq, origin).wait_recv()

    def q_part(target):
        return q_mid.at[lane(target % 4, 128), lane(target // 4, HD)]

    for d in range(1, 16):
        target = (seq + d) % 16
        go(remote(q_part(target), q_out.at[seq], qb_send.at[d], qb_recv.at[d], target, ctx))
    own_qb = pltpu.make_async_copy(q_part(seq), q_out.at[seq], local_sem.at[4])
    own_qb.start()

    for j in range(2):
        for i in range(2):
            p1_in(i, j).wait_recv()
            go(p1(i, 2 + j))
            go(p2(i, 1 + j, 0))
            go(p2(i, 1 + j, 1))
    for j in range(2):
        for i in range(2):
            p2_in(i, 0, j).wait_recv()
            go(p2(i, 0, 2 + j))
    for i in range(2):
        p1_in(i, 2).wait_recv()
        p1_in(i, 3).wait_recv()
        go(p2(i, 3, 0))
        go(p2(i, 3, 1))
    for p in (1, 2):
        for j in range(2):
            for i in range(2):
                p2_in(i, p, j).wait_recv()
                go(p2(i, p, 2 + j))

    own_c.wait()
    for d in range(1, 8):
        origin = (ctx - d + 8) % 8
        remote(
            packed.at[pl.ds(ctx * GROUP * CAP, GROUP * CAP)],
            arrived.at[pl.ds(origin * GROUP * CAP, GROUP * CAP)],
            c_send.at[d], c_recv.at[d], seq, origin,
        ).wait_recv()

    def ckv_part(dx, dz, half=None):
        index = (x + dx + 4) % 4 * 4 + (z + dz + 4) % 4
        if half is None:
            return ckv_out.at[:, index]
        return ckv_out.at[:, index, pl.ds(half * 16, 16)]

    def squeeze(member):
        def body(step, carry):
            for k in range(8):
                n = step * 8 + k
                block = arrived[places_ref[member * NSEL + n]]
                compact[member, 0, n] = block[0]
                compact[member, 1, n] = block[1]
            return carry

        lax.fori_loop(0, NSEL // 8, body, 0)

    for dz in (2, 1, 3, 0):
        member = (z + dz) % 4
        squeeze(member)
        if dz:
            go(remote(compact.at[member], ckv_part(0, 0), cz_send.at[dz], cz_recv.at[dz], member * 4 + x, ctx))
        else:
            own_z = pltpu.make_async_copy(compact.at[member], ckv_part(0, 0), local_sem.at[5])
            own_z.start()

    for j in range(2):
        for i in range(2):
            p2_in(i, 3, j).wait_recv()
            go(p2(i, 3, 2 + j))

    def cx(dz, j):
        step, block, half = first_hop(0, j)
        ref = ckv_part(block, dz, half)
        return remote(ref, ref, cx_send.at[dz, j], cx_recv.at[dz, j], along("x", step), ctx)

    def cx_in(dz, j):
        step, block, half = first_hop(0, j)
        ref = ckv_part(block - step, dz, half)
        return remote(ref, ref, cx_send.at[dz, j], cx_recv.at[dz, j], along("x", step), ctx)

    order = (0, 3, 1, 2)
    for dz in order:
        if dz:
            ref = ckv_part(0, -dz)
            remote(compact.at[0], ref, cz_send.at[dz], cz_recv.at[dz], along("z", -dz), ctx).wait_recv()
        else:
            own_z.wait()
        go(cx((4 - dz) % 4, 0))
        go(cx((4 - dz) % 4, 1))
    for dz in order:
        for j in range(2):
            cx_in((4 - dz) % 4, j).wait_recv()
            go(cx((4 - dz) % 4, 2 + j))

    for p in range(4):
        for i in range(2):
            p2_in(i, p, 2).wait_recv()
            p2_in(i, p, 3).wait_recv()
    own_qb.wait()
    for d in range(1, 16):
        origin = (seq - d + 16) % 16
        remote(q_part(seq), q_out.at[origin], qb_send.at[d], qb_recv.at[d], origin, ctx).wait_recv()
    for dz in order:
        for j in (2, 3):
            cx_in((4 - dz) % 4, j).wait_recv()
    for copy in sends:
        copy.wait_send()


def exchange(send_rows, places, queries, stretch, cache):
    any_space = pl.BlockSpec(memory_space=pl.ANY)
    smem = pl.BlockSpec(memory_space=pltpu.SMEM)
    dma = pltpu.SemaphoreType.DMA
    bf16 = jnp.bfloat16
    return pl.pallas_call(
        comm_kernel,
        in_specs=[smem, smem, any_space, any_space, any_space],
        out_specs=[any_space] * 3,
        out_shape=[
            jax.ShapeDtypeStruct((16, 128, HD), bf16),
            jax.ShapeDtypeStruct((2, STRETCH, HD), bf16),
            jax.ShapeDtypeStruct((2, 16, NSEL, 8, HD), bf16),
        ],
        scratch_shapes=[
            pltpu.VMEM(cache.shape, bf16),
            pltpu.VMEM((H * CAP, 2, 8, HD), bf16),
            pltpu.VMEM((H * CAP, 2, 8, HD), bf16),
            pltpu.VMEM((GROUP, 2, NSEL, 8, HD), bf16),
            pltpu.VMEM((8 * TOK, GROUP * HD), bf16),
            dma((8,)), dma((8,)), dma((8,)), dma((8,)), dma((8,)), dma((8,)), dma((16,)), dma((16,)),
            dma((2, 4)), dma((2, 4)), dma((2, 4, 4)), dma((2, 4, 4)), dma((4,)), dma((4,)), dma((4, 4)), dma((4, 4)),
            dma((6,)),
        ],
        compiler_params=pltpu.CompilerParams(collective_id=0, has_side_effects=True, vmem_limit_bytes=40 << 20),
    )(send_rows, places, queries, stretch, cache)


def attend(q, carry, keys, values, limit):
    peak, acc = carry
    scores = lax.dot_general(q, keys, (((1,), (1,)), ((), ())), preferred_element_type=jnp.float32)
    if limit is not None:
        scores = jnp.where(lax.broadcasted_iota(jnp.int32, scores.shape, 1) <= limit, scores, masked_value)
    new_peak = jnp.maximum(peak, jnp.max(scores, axis=1, keepdims=True))
    weights = jnp.exp2((scores - new_peak) * EXP_SCALE)
    fading = jnp.exp2((peak - new_peak) * EXP_SCALE)
    mixed = jnp.dot(
        weights.astype(jnp.bfloat16),
        jnp.concatenate([values, jnp.ones((keys.shape[0], HD), jnp.bfloat16)], axis=1),
        preferred_element_type=jnp.float32,
    )
    return new_peak, acc * fading + mixed


def flash_kernel(q_ref, kv_ref, ckv_ref, out_ref, own, send_sem, recv_sem, local_sem):
    seq, ctx = lax.axis_index("seq"), lax.axis_index("ctx")
    member, quarter = seq // 4, seq % 4
    head = ctx * GROUP + member

    barrier = pltpu.get_barrier_semaphore()
    for other in range(GROUP):
        for group in range(KVH):
            origin = other * 4 + ctx // 2

            @pl.when((origin != seq) | (group != ctx))
            def _(origin=origin, group=group):
                pl.semaphore_signal(barrier, inc=1, device_id=(origin, group), device_id_type=MESH)

    mine = quarter == ctx // 2

    def column(index):
        return pl.ds(pl.multiple_of(index * HD, HD), HD)

    def give(piece, half):
        source = own.at[piece, pl.ds(half * TOK, TOK), :]
        return remote(
            source, out_ref.at[:, column(head)], send_sem.at[piece, half], recv_sem.at[member, ctx],
            piece, quarter * 2 + half,
        )

    def is_self(piece, half):
        return (piece == seq) & (quarter * 2 + half == ctx)

    row = lax.broadcasted_iota(jnp.int32, (Q_TILE, 1), 0)
    limit = row // 128 * 512 + quarter * 128 + row % 128

    for tile in reversed(range(16 * 128 // Q_TILE)):
        q = q_ref[pl.ds(tile * Q_TILE, Q_TILE), :]
        carry = (
            jnp.full((Q_TILE, 1), masked_value, jnp.float32),
            jnp.zeros((Q_TILE, 2 * HD), jnp.float32),
        )

        def cached(block, carry, q=q):
            rows = pl.ds(pl.multiple_of(block * K_TILE, K_TILE), K_TILE)
            return attend(q, carry, ckv_ref[0, rows, :], ckv_ref[1, rows, :], None)

        def full(block, carry, q=q):
            rows = pl.ds(pl.multiple_of(block * K_TILE, K_TILE), K_TILE)
            return attend(q, carry, kv_ref[0, rows, :], kv_ref[1, rows, :], None)

        carry = lax.fori_loop(0, CACHED // K_TILE, cached, carry)
        carry = lax.fori_loop(0, tile, full, carry)
        rows = pl.ds(tile * K_TILE, K_TILE)
        peak, acc = attend(q, carry, kv_ref[0, rows, :], kv_ref[1, rows, :], limit)
        own[pl.ds(tile * 2, 2)] = (acc[:, :HD] / acc[:, HD:]).astype(jnp.bfloat16).reshape(2, 128, HD)
        if tile == 16 * 128 // Q_TILE - 1:
            pl.semaphore_wait(barrier, 32 - mine.astype(jnp.int32))
        for piece in (2 * tile, 2 * tile + 1):
            for half in range(2):
                @pl.when(jnp.logical_not(is_self(piece, half)))
                def _(piece=piece, half=half):
                    give(piece, half).start()

                @pl.when(is_self(piece, half))
                def _(piece=piece, half=half):
                    pltpu.make_async_copy(
                        own.at[piece, pl.ds(half * TOK, TOK), :], out_ref.at[:, column(head)], local_sem
                    ).start()

    for piece in range(16):
        for half in range(2):
            @pl.when(jnp.logical_not(is_self(piece, half)))
            def _(piece=piece, half=half):
                give(piece, half).wait_send()

            @pl.when(is_self(piece, half))
            def _(piece=piece, half=half):
                pltpu.make_async_copy(
                    own.at[piece, pl.ds(half * TOK, TOK), :], out_ref.at[:, column(head)], local_sem
                ).wait()
    for other in range(GROUP):
        for group in range(KVH):
            origin = other * 4 + ctx // 2

            @pl.when((origin != seq) | (group != ctx))
            def _(other=other, group=group, origin=origin):
                remote(
                    own.at[0, pl.ds(0, TOK), :], out_ref.at[:, pl.ds((group * GROUP + other) * HD, HD)],
                    send_sem.at[0, 0], recv_sem.at[other, group], origin, group,
                ).wait_recv()


def flash(q, kv, ckv):
    vmem = pl.BlockSpec(memory_space=pltpu.VMEM)
    dma = pltpu.SemaphoreType.DMA
    return pl.pallas_call(
        flash_kernel,
        in_specs=[vmem] * 3,
        out_specs=pl.BlockSpec(memory_space=pl.ANY),
        out_shape=jax.ShapeDtypeStruct((TOK, H * HD), jnp.bfloat16),
        scratch_shapes=[
            pltpu.VMEM((16, 128, HD), jnp.bfloat16),
            dma((16, 2)), dma((GROUP, KVH)), dma,
        ],
        compiler_params=pltpu.CompilerParams(collective_id=1, has_side_effects=True, vmem_limit_bytes=48 << 20),
    )(q, kv, ckv)


def block_places(vertical, slash, owner_map, ctx_index):
    nblk = owner_map.shape[0]
    selected = jnp.concatenate([vertical, nblk - 1 - slash], axis=1)
    hit = selected[:, :, None] == jnp.arange(nblk, dtype=jnp.int32)
    storage = jnp.sum(jnp.where(hit, owner_map, 0), axis=2)
    per_ctx = nblk // 8
    owner = storage // per_ctx
    local_row = storage % per_ctx
    order = jnp.arange(NSEL, dtype=jnp.int32)
    earlier = (owner[:, :, None] == owner[:, None, :]) & (order[None, None, :] < order[None, :, None])
    rank = jnp.sum(earlier.astype(jnp.int32), axis=2)
    slot_hit = (owner[:, :, None] == ctx_index) & (rank[:, :, None] == jnp.arange(CAP, dtype=jnp.int32))
    send_rows = jnp.sum(jnp.where(slot_hit, local_row[:, :, None], 0), axis=1)
    in_group = jnp.arange(H, dtype=jnp.int32)[:, None] % GROUP
    places = (owner * GROUP + in_group) * CAP + rank
    return send_rows, places


def on_device(queries, stretch_kv, cache_kv, vertical, slash, owner_map):
    ctx_index = lax.axis_index("ctx")
    send_rows, places = block_places(vertical, slash, owner_map, ctx_index)
    own_places = lax.dynamic_slice_in_dim(places, ctx_index * GROUP, GROUP, 0)
    q, kv, ckv = exchange(send_rows.reshape(-1), own_places.reshape(-1), queries, stretch_kv, cache_kv)
    return flash(q.reshape(16 * 128, HD), kv, ckv.reshape(2, CACHED, HD))


def solution(mesh):
    placed = (
        P(("seq", "ctx"), None),
        P(None, ("seq", "ctx"), None),
        P("ctx", None, None, "seq", None),
        P(),
        P(),
        P(),
    )
    return jax.shard_map(
        on_device, mesh=mesh, in_specs=placed, out_specs=P(("seq", "ctx"), None), check_vma=False
    )
```

time: 233 us -> 145 us (0.62)
  Pallas kernels: 47.1 us -> 132 us
  blocking collectives: 84.2 us -> 0 us
  waiting for transfers between devices: 63.8 us -> 0 us
  between operations: 13.6 us -> 0.07 us
  local copies, waits for them, and re-layouts: 13.7 us -> 7.32 us
  starting transfers between devices: 4.76 us -> 0 us
    pallas_call x1 -> x2, Pallas kernels: 47.1 us -> 132 us  [the longest x1 66.6 us: flash(): pl.pallas_call(flash_kernel, in_specs=[vmem] * 3, out_specs=pl.BlockSpec(...]
    all_to_all x6 -> x0, blocking collectives: 84.2 us -> none  [the longest x1 16.6 us: on_device(): lax.all_to_all(out.reshape(16, 2 * TOK, HD), 'seq', split_axis=0, concat_...]
    all_gather x2 -> x0, waiting for transfers between devices: 42.5 us -> none  [the longest x1 42.5 us: on_device(): kv = lax.all_gather(own_kv, 'seq', axis=1, tiled=True)]
    all_to_all x1 -> x0, waiting for transfers between devices: 21.3 us -> none  [on_device(): lax.all_to_all(packed, 'ctx', split_axis=0, concat_axis=0, tiled=True)]
    gather x2 -> x0, local copies, waits for them, and re-layouts: 6.88 us -> none  [the longest x1 6.18 us: on_device(): packed = cache_kv[send_rows, :, group_of]]
    all_to_all x1 -> x0, starting transfers between devices: 4.69 us -> none  [on_device(): lax.all_to_all(packed, 'ctx', split_axis=0, concat_axis=0, tiled=True)]
    unnamed x11 -> x9, local copies, waits for them, and re-layouts: 3.68 us -> 6.89 us
  transfers between devices with their start and end apart: 3 -> 0, of which waited for: 2 -> 0; matrix products, arithmetic and copies ran while one was open for 1% -> 0% of each run, Pallas kernels for 0% -> 0%
where the time goes in v2:
time: 145 us; the launch traced here: 144 us
  Pallas kernels  132 us (91%)
  local copies, waits for them, and re-layouts  7.32 us (5%)
  other arithmetic  4.13 us (3%)
    pallas_call x1, Pallas kernels, flash(): pl.pallas_call(flash_kernel, in_specs=[vmem] * 3, out_specs=pl.BlockSpec(...  66.6 us
    pallas_call x1, Pallas kernels, exchange(): pl.pallas_call(comm_kernel, in_specs=[smem, smem, any_space, any_space, a...  65.6 us
    unnamed x9, local copies, waits for them, and re-layouts  6.89 us

profile of v2, /device:TPU:0, one launch (start us, length us, event | category | flops | bytes accessed | tf_op | source)
XLA Modules:
  0.0 143.7 jit_solution(2164794151780572413)
XLA Ops:
  0.0 0.1 dynamic-slice
  0.1 0.7 broadcast_subtract_fusion
  0.8 0.7 pad_add_fusion
  1.5 0.1 copy.9
  1.6 1.6 %select_reduce_fusion = s32[32,32]{1,0:T(8,128)S(1)} fusion(s32[1024]{0:T(1024)} %param.11, s32[32,32]{1,0:T(8,128)S(1)} %copy.9), kind=kLoop, calls=%fused_computation | loop fusion | flops 3144704 | bytes 12288 | tf_op jit(solution)/shard_map/reduce_sum | solution.py:432
  3.2 0.8 convert_reduce_fusion
  4.0 0.1 dynamic-slice_add_fusion
  4.0 0.3 select_reduce_fusion.1
  4.3 0.1 reshape.96.places_ref
  4.4 0.1 copy.10
  4.5 0.1 reshape.95.rows_ref
  4.6 0.0 copy-start.1
  4.6 2.2 %copy-done.1 = bf16[128,2,8,8,128]{4,3,2,1,0:T(8,128)(2,1)S(1)} copy-done((bf16[128,2,8,8,128]{4,3,2,1,0:T(8,128)(2,1)S(1)}, bf16[128,2,8,8,128]{4,3,2,1,0:T(8,128)(2,1)}, u32[]{:S(2)}) %copy-start.1) | copy-done | bytes 4194328
  6.8 0.0 copy-start.2
  6.8 1.0 copy-done.2
  7.8 0.0 copy-start.3
  7.8 0.9 copy-done.3
  8.8 65.6 %shard_map.64 = (bf16[16,128,128]{2,1,0:T(8,128)(2,1)S(1)}, bf16[2,8192,128]{2,1,0:T(8,128)(2,1)S(1)}, bf16[2,16,32,8,128]{4,3,2,1,0:T(8,128)(2,1)S(1)}) custom-call(s32[384]{0:T(512)S(1)} %reshape.95.rows_ref, s32[128]{0:T(128)S(1)} %reshape.96.places_ref, bf16[64,4096]{1,0:T(8,128)(2,1)S(1)} %copy-done.2, bf16[2,64,1024]{2,1,0:T(8,128)(2,1)S(1)} %copy-done.3, ...), custom_call_target="tpu_custom_call" | custom-call | tf_op jit(solution)/shard_map/pallas_call | solution.py:284
  74.4 0.0 copy-start
  74.4 1.9 %copy-done = bf16[2,8192,128]{2,1,0:T(8,128)(2,1)} copy-done((bf16[2,8192,128]{2,1,0:T(8,128)(2,1)}, bf16[2,8192,128]{2,1,0:T(8,128)(2,1)S(1)}, u32[]{:S(2)}) %copy-start) | copy-done | bytes 4194328
  76.3 66.6 %shard_map.65 = bf16[64,4096]{1,0:T(8,128)(2,1)S(1)} custom-call(bf16[2048,128]{1,0:T(8,128)(2,1)S(1)} %bitcast.3, bf16[2,8192,128]{2,1,0:T(8,128)(2,1)} %copy-done, bf16[2,4096,128]{2,1,0:T(8,128)(2,1)S(1)} %bitcast.2), custom_call_target="tpu_custom_call" | custom-call | tf_op jit(solution)/shard_map/pallas_call | solution.py:415
  142.9 0.8 copy.12
  (3 shorter events, 0.0 us)
Async XLA Ops:
  4.6 2.2 %copy-start.1 = (bf16[128,2,8,8,128]{4,3,2,1,0:T(8,128)(2,1)S(1)}, bf16[128,2,8,8,128]{4,3,2,1,0:T(8,128)(2,1)}, u32[]{:S(2)}) copy-start(bf16[128,2,8,8,128]{4,3,2,1,0:T(8,128)(2,1)} %cache.1) | copy-start | bytes 12582916
  6.8 1.0 copy-start.2
  7.8 0.9 copy-start.3
  74.4 1.9 %copy-start = (bf16[2,8192,128]{2,1,0:T(8,128)(2,1)}, bf16[2,8192,128]{2,1,0:T(8,128)(2,1)S(1)}, u32[]{:S(2)}) copy-start(bf16[2,8192,128]{2,1,0:T(8,128)(2,1)S(1)} %get-tuple-element.9.kv_ref) | copy-start | bytes 12582916
